TPU v7x, 256 devices: a whole 4x4x8 slice. The times are simulated.
256 devices in a mesh: group: 8 (over x, core), prompt: 32 (over z, y).
Axes of the slice: x: 4, y: 4, z: 8, core: 2. Of those that a mesh axis runs over, the one named last changes fastest.
Arguments:
- queries: bfloat16 [32, 8, 64, 3072], P('prompt', 'group'), may hold values from -48 to 48
- fresh_latent: bfloat16 [32, 8, 64, 576], P('prompt', 'group'), may hold values from -6 to 6
- latent_cache: bfloat16 [32, 8, 512, 576], P('prompt', 'group'), may hold values from -48 to 48
- selected: int32 [32, 8, 64], P('prompt', 'group'), may hold values from 0 to 511, as said below
- position: int32 [32, 8], P('prompt'), may hold values from 0 to 7, each once within a row
- latent_gain: bfloat16 [512], replicated, may hold values from 0.099609375 to 1.8984375
- kv_up: bfloat16 [512, 4096], P('prompt'), may hold values from -0.25 to 0.25
- out_weight: bfloat16 [2048, 2048], P('prompt'), may hold values from -0.125 to 0.125
Outputs:
- attended: bfloat16 [32, 8, 64, 2048], P('prompt', 'group')
- blended: bfloat16 [32, 8, 512, 576], P('prompt', 'group')
Inputs may be any that keep to these rules, and one draw needn't show every extreme that they name: `selected`: the 64 indices of a group are distinct and increasing.
All inputs are finite; a program needn't handle non-finite values.
Results may differ from a plain program's by a relative error of at most 0.011.
Values may be sent and summed in bfloat16 or wider, within the bound.
A program may use at most 128 MiB of HBM per device.

v0:
```python
import jax
import jax.numpy as jnp
from jax import lax
from jax.sharding import Mesh
from jax.sharding import PartitionSpec as P

D = 2048
H = 16
DN = 128
DR = 64
DV = 128
LAT = 512
PROMPT = ("prompt_0", "prompt_1")


def whole_of(array, axes, dim):
    whole = array
    for number in range(len(axes) - 1, -1, -1):
        whole = lax.all_gather(whole, axes[number], axis=dim, tiled=True)
    return whole


def rope_rotate(values, places):
    half = values.shape[-1] // 2
    freqs = 10000.0 ** (-jnp.arange(half, dtype=jnp.float32) / half)
    angles = places[..., None] * freqs
    cosine = jnp.cos(angles)
    sine = jnp.sin(angles)
    first = values[..., :half]
    second = values[..., half:]
    return jnp.concatenate([first * cosine - second * sine, second * cosine + first * sine], -1)


def prepare_rows(fresh, gain, places):
    latent = fresh[..., :LAT].astype(jnp.float32)
    factor = lax.rsqrt(jnp.mean(latent * latent, -1, keepdims=True) + 1e-06)
    normed = latent * factor * gain.astype(jnp.float32)
    turned = rope_rotate(fresh[..., LAT:].astype(jnp.float32), places)
    return jnp.concatenate([normed, turned], -1).astype(jnp.bfloat16)


def shards(queries, fresh_latent, latent_cache, selected, position, latent_gain, kv_up, out_weight):
    prompts, groups, picks, _ = queries.shape
    length = latent_cache.shape[2]
    first_group = lax.axis_index("group") * groups
    own_order = lax.dynamic_slice_in_dim(position, first_group, groups, 1)
    place_int = own_order[:, :, None] * length + selected
    places = place_int.astype(jnp.float32)
    fresh_rows = prepare_rows(fresh_latent, latent_gain, places)
    prompt_ids = jnp.arange(prompts, dtype=jnp.int32)[:, None, None]
    group_ids = jnp.arange(groups, dtype=jnp.int32)[None, :, None]
    blended = latent_cache.at[prompt_ids, group_ids, selected].set(fresh_rows)
    whole_kv = whole_of(kv_up, PROMPT, 0).reshape(LAT, H, DN + DV)
    shaped = queries.reshape(prompts, groups, picks, H, DN + DR)
    absorbed = jnp.einsum(
        "pcshd,lhd->pcshl", shaped[..., :DN], whole_kv[..., :DN], preferred_element_type=jnp.float32
    ).astype(jnp.bfloat16)
    turned = rope_rotate(shaped[..., DN:].astype(jnp.float32), places[..., None]).astype(
        jnp.bfloat16
    )
    rows = groups * picks
    query_vec = jnp.concatenate([absorbed, turned], -1).reshape(prompts, rows, H, LAT + DR)
    query_place = place_int.reshape(prompts, rows)
    scale = (DN + DR) ** (-0.5)
    offsets = jnp.arange(length, dtype=jnp.int32)

    def update(state, keys, key_place):
        peak, total, mixed = state
        allowed = (key_place[:, None, :] <= query_place[:, :, None])[:, :, None, :]
        scores = (
            jnp.einsum("pqhe,pke->pqhk", query_vec, keys, preferred_element_type=jnp.float32)
            * scale
        )
        block_peak = jnp.max(jnp.where(allowed, scores, -1e30), -1)
        new_peak = jnp.maximum(peak, block_peak)
        probs = jnp.where(allowed, jnp.exp(scores - new_peak[..., None]), 0.0)
        decay = jnp.exp(peak - new_peak)
        total = total * decay + jnp.sum(probs, -1)
        mixed = mixed * decay[..., None] + jnp.einsum(
            "pqhk,pkl->pqhl",
            probs.astype(jnp.bfloat16),
            keys[..., :LAT],
            preferred_element_type=jnp.float32,
        )
        return (new_peak, total, mixed)

    start_state = (
        jnp.full((prompts, rows, H), -1e30, jnp.float32),
        jnp.zeros((prompts, rows, H), jnp.float32),
        jnp.zeros((prompts, rows, H, LAT), jnp.float32),
    )
    piece = lax.all_gather(blended, "group", axis=1, tiled=True)

    def one_group(index, carry):
        keys = lax.dynamic_slice_in_dim(piece, index, 1, 1)[:, 0]
        order = lax.dynamic_slice_in_dim(position, index, 1, 1)
        key_place = order * length + offsets[None, :]
        needed = jnp.any(key_place[:, :1] <= jnp.max(query_place, -1, keepdims=True))
        return lax.cond(needed, lambda c: update(c, keys, key_place), lambda c: c, carry)

    peak, total, mixed = lax.fori_loop(0, piece.shape[1], one_group, start_state)
    latent_mix = (mixed / total[..., None]).astype(jnp.bfloat16)
    heads = jnp.einsum(
        "pqhl,lhv->pqhv", latent_mix, whole_kv[..., DN:], preferred_element_type=jnp.float32
    ).astype(jnp.bfloat16)
    heads = heads.reshape(prompts * rows, H * DV)
    whole_out = lax.all_gather(out_weight, PROMPT, axis=0, tiled=True)
    attended = jnp.dot(heads, whole_out, preferred_element_type=jnp.float32)
    return (attended.astype(jnp.bfloat16).reshape(prompts, groups, picks, D), blended)


def solution(mesh):
    split = Mesh(mesh.devices.reshape(mesh.shape["group"], 8, 4), ("group", "prompt_0", "prompt_1"))
    return jax.shard_map(
        shards,
        mesh=split,
        in_specs=(
            P(PROMPT, "group", None, None),
            P(PROMPT, "group", None, None),
            P(PROMPT, "group", None, None),
            P(PROMPT, "group", None),
            P(PROMPT, None),
            P(),
            P(PROMPT, None),
            P(PROMPT, None),
        ),
        out_specs=(P(PROMPT, "group", None, None), P(PROMPT, "group", None, None)),
        check_vma=False,
    )
```

profile of v0, /device:TPU:57, one launch (start us, length us, event | category | flops | bytes accessed | tf_op | source)
XLA Modules:
  0.0 239.9 jit_solution(15318648085517091847)
XLA Ops:
  7.2 10.8 %all_gather.13 = bf16[64,4096]{1,0:T(8,128)(2,1)} all-gather(bf16[16,4096]{1,0:T(8,128)(2,1)} %param.18), channel_id=1, replica_groups=mesh['group'=8,'prompt_0'=8,'prompt_1'=4] {'prompt_1'}, dimensions={0}, use_global_device_ids=true | all-gather | bytes 655360 | tf_op jit(solution)/shard_map/all_gather | solution.py:19
  29.4 46.8 %all-gather.5.cloned.1.call-done = bf16[512,4096]{1,0:T(8,128)(2,1)} async-done(((bf16[64,4096]{1,0:T(8,128)(2,1)}), bf16[512,4096]{1,0:T(8,128)(2,1)}) %all-gather.5.cloned.1.call-update) | async-done | bytes 4194320 | tf_op jit(solution)/shard_map/all_gather | solution.py:19
  76.2 6.5 %copy.53 = bf16[512,4096]{0,1:T(8,128)(2,1)} copy(bf16[512,4096]{1,0:T(8,128)(2,1)} %all-gather.5.cloned.1.call-done) | data formatting | bytes 8388608 | tf_op jit(solution)/shard_map/all_gather | solution.py:19
  86.1 31.9 %all-gather.9.cloned.1.call-done = bf16[4096,576]{1,0:T(8,128)(2,1)} async-done(((bf16[512,576]{1,0:T(8,128)(2,1)}), bf16[4096,576]{1,0:T(8,128)(2,1)}) %all-gather.9.cloned.1.call-update) | async-done | bytes 4718608 | tf_op jit(solution)/shard_map/all_gather | solution.py:92
  118.0 7.7 %copy.57 = bf16[1,8,512,576]{2,3,1,0:T(8,128)(2,1)} copy(bf16[1,8,512,576]{3,2,1,0:T(8,128)(2,1)} %bitcast.103) | data formatting | bytes 9437184
  126.3 98.4 %while.20 = (s32[]{:T(128)}, f32[1,64,16]{1,2,0:T(8,128)S(1)}, f32[1,64,16]{1,2,0:T(8,128)S(1)}, f32[1,64,16,512]{3,2,1,0:T(8,128)S(1)}, s32[1,8]{1,0:T(1,128)S(...) while((s32[]{:T(128)}, f32[1,64,16]{1,2,0:T(8,128)S(1)}, ...), condition=%wide.region_8.9_spmd.clone, body=%wide.region_3.8_spmd.clone.sunk | while | flops 1146129920 | bytes 17670692 | solution.py:101
  129.5 9.0 %conditional.3 = ((f32[1,64,16]{1,2,0:T(8,128)S(1)}, f32[1,64,16]{1,2,0:T(8,128)S(1)}, f32[1,64,16,512]{3,2,1,0:T(8,128)S(1)})) conditional(s32[]{:T(128)} %bitcast.97, (f32[1,64,16]{1,2,0:T(8,128)S(1)}, f32[1,64,16]{1,2,0:T(8,128)S(1)}, f32[1,64,16,512]{3,2,1,0:T(8,128)S(1)}) %tuple.70, (s32[1,512]{1,0:T(1,128)S(1)}, s32[1,1,64]{2,1,0:T(1,128)S(1)}, ...), branch_computations={%region_4.0_spmd, %region_5.7_spmd} | conditional | flops 1146129408 | bytes 17668416 | solution.py:99
  130.8 2.5 %fusion.2 = (f32[64,16]{0,1:T(8,128)S(1)}, f32[512,64,16]{0,1,2:T(8,128)S(1)}) fusion(pred[64,512]{1,0:T(8,128)(4,1)S(1)} %broadcast_compare_fusion, bf16[1,64,16,576]{3,1,2,0:T(8,128)(2,1)} %get-tuple-element.279, bf16[1,1,512,576]{2,3,1,0:T(8,128)(2,1)S(1)} %constant_dynamic-slice_fusion), kind=kOutput, calls=%fused_computation.5 | convolution fusion | flops 605551616 | bytes 3903488 | tf_op jit(solution)/shard_map/while/body/eval_jaxpr/cond/branch_1_fun/pqhe,pke->pqhk/dot_general | solution.py:71
  136.3 2.2 bitcast_add_fusion
  141.8 9.1 %conditional.3 = ((f32[1,64,16]{1,2,0:T(8,128)S(1)}, f32[1,64,16]{1,2,0:T(8,128)S(1)}, f32[1,64,16,512]{3,2,1,0:T(8,128)S(1)})) conditional(s32[]{:T(128)} %bitcast.97, (f32[1,64,16]{1,2,0:T(8,128)S(1)}, f32[1,64,16]{1,2,0:T(8,128)S(1)}, f32[1,64,16,512]{3,2,1,0:T(8,128)S(1)}) %tuple.70, (s32[1,512]{1,0:T(1,128)S(1)}, s32[1,1,64]{2,1,0:T(1,128)S(1)}, ...), branch_computations={%region_4.0_spmd, %region_5.7_spmd} | conditional | flops 1146129408 | bytes 17668416 | solution.py:99
  143.1 2.5 %fusion.2 = (f32[64,16]{0,1:T(8,128)S(1)}, f32[512,64,16]{0,1,2:T(8,128)S(1)}) fusion(pred[64,512]{1,0:T(8,128)(4,1)S(1)} %broadcast_compare_fusion, bf16[1,64,16,576]{3,1,2,0:T(8,128)(2,1)} %get-tuple-element.279, bf16[1,1,512,576]{2,3,1,0:T(8,128)(2,1)S(1)} %constant_dynamic-slice_fusion), kind=kOutput, calls=%fused_computation.5 | convolution fusion | flops 605551616 | bytes 3903488 | tf_op jit(solution)/shard_map/while/body/eval_jaxpr/cond/branch_1_fun/pqhe,pke->pqhk/dot_general | solution.py:71
  154.1 9.0 %conditional.3 = ((f32[1,64,16]{1,2,0:T(8,128)S(1)}, f32[1,64,16]{1,2,0:T(8,128)S(1)}, f32[1,64,16,512]{3,2,1,0:T(8,128)S(1)})) conditional(s32[]{:T(128)} %bitcast.97, (f32[1,64,16]{1,2,0:T(8,128)S(1)}, f32[1,64,16]{1,2,0:T(8,128)S(1)}, f32[1,64,16,512]{3,2,1,0:T(8,128)S(1)}) %tuple.70, (s32[1,512]{1,0:T(1,128)S(1)}, s32[1,1,64]{2,1,0:T(1,128)S(1)}, ...), branch_computations={%region_4.0_spmd, %region_5.7_spmd} | conditional | flops 1146129408 | bytes 17668416 | solution.py:99
  155.4 2.5 %fusion.2 = (f32[64,16]{0,1:T(8,128)S(1)}, f32[512,64,16]{0,1,2:T(8,128)S(1)}) fusion(pred[64,512]{1,0:T(8,128)(4,1)S(1)} %broadcast_compare_fusion, bf16[1,64,16,576]{3,1,2,0:T(8,128)(2,1)} %get-tuple-element.279, bf16[1,1,512,576]{2,3,1,0:T(8,128)(2,1)S(1)} %constant_dynamic-slice_fusion), kind=kOutput, calls=%fused_computation.5 | convolution fusion | flops 605551616 | bytes 3903488 | tf_op jit(solution)/shard_map/while/body/eval_jaxpr/cond/branch_1_fun/pqhe,pke->pqhk/dot_general | solution.py:71
  160.9 2.2 bitcast_add_fusion
  166.4 9.2 %conditional.3 = ((f32[1,64,16]{1,2,0:T(8,128)S(1)}, f32[1,64,16]{1,2,0:T(8,128)S(1)}, f32[1,64,16,512]{3,2,1,0:T(8,128)S(1)})) conditional(s32[]{:T(128)} %bitcast.97, (f32[1,64,16]{1,2,0:T(8,128)S(1)}, f32[1,64,16]{1,2,0:T(8,128)S(1)}, f32[1,64,16,512]{3,2,1,0:T(8,128)S(1)}) %tuple.70, (s32[1,512]{1,0:T(1,128)S(1)}, s32[1,1,64]{2,1,0:T(1,128)S(1)}, ...), branch_computations={%region_4.0_spmd, %region_5.7_spmd} | conditional | flops 1146129408 | bytes 17668416 | solution.py:99
  167.6 2.5 %fusion.2 = (f32[64,16]{0,1:T(8,128)S(1)}, f32[512,64,16]{0,1,2:T(8,128)S(1)}) fusion(pred[64,512]{1,0:T(8,128)(4,1)S(1)} %broadcast_compare_fusion, bf16[1,64,16,576]{3,1,2,0:T(8,128)(2,1)} %get-tuple-element.279, bf16[1,1,512,576]{2,3,1,0:T(8,128)(2,1)S(1)} %constant_dynamic-slice_fusion), kind=kOutput, calls=%fused_computation.5 | convolution fusion | flops 605551616 | bytes 3903488 | tf_op jit(solution)/shard_map/while/body/eval_jaxpr/cond/branch_1_fun/pqhe,pke->pqhk/dot_general | solution.py:71
  171.0 2.3 copy.47
  173.3 2.2 bitcast_add_fusion
  178.8 9.1 %conditional.3 = ((f32[1,64,16]{1,2,0:T(8,128)S(1)}, f32[1,64,16]{1,2,0:T(8,128)S(1)}, f32[1,64,16,512]{3,2,1,0:T(8,128)S(1)})) conditional(s32[]{:T(128)} %bitcast.97, (f32[1,64,16]{1,2,0:T(8,128)S(1)}, f32[1,64,16]{1,2,0:T(8,128)S(1)}, f32[1,64,16,512]{3,2,1,0:T(8,128)S(1)}) %tuple.70, (s32[1,512]{1,0:T(1,128)S(1)}, s32[1,1,64]{2,1,0:T(1,128)S(1)}, ...), branch_computations={%region_4.0_spmd, %region_5.7_spmd} | conditional | flops 1146129408 | bytes 17668416 | solution.py:99
  180.0 2.5 %fusion.2 = (f32[64,16]{0,1:T(8,128)S(1)}, f32[512,64,16]{0,1,2:T(8,128)S(1)}) fusion(pred[64,512]{1,0:T(8,128)(4,1)S(1)} %broadcast_compare_fusion, bf16[1,64,16,576]{3,1,2,0:T(8,128)(2,1)} %get-tuple-element.279, bf16[1,1,512,576]{2,3,1,0:T(8,128)(2,1)S(1)} %constant_dynamic-slice_fusion), kind=kOutput, calls=%fused_computation.5 | convolution fusion | flops 605551616 | bytes 3903488 | tf_op jit(solution)/shard_map/while/body/eval_jaxpr/cond/branch_1_fun/pqhe,pke->pqhk/dot_general | solution.py:71
  183.4 2.2 copy.47
  185.6 2.2 bitcast_add_fusion
  191.1 9.1 %conditional.3 = ((f32[1,64,16]{1,2,0:T(8,128)S(1)}, f32[1,64,16]{1,2,0:T(8,128)S(1)}, f32[1,64,16,512]{3,2,1,0:T(8,128)S(1)})) conditional(s32[]{:T(128)} %bitcast.97, (f32[1,64,16]{1,2,0:T(8,128)S(1)}, f32[1,64,16]{1,2,0:T(8,128)S(1)}, f32[1,64,16,512]{3,2,1,0:T(8,128)S(1)}) %tuple.70, (s32[1,512]{1,0:T(1,128)S(1)}, s32[1,1,64]{2,1,0:T(1,128)S(1)}, ...), branch_computations={%region_4.0_spmd, %region_5.7_spmd} | conditional | flops 1146129408 | bytes 17668416 | solution.py:99
  192.3 2.6 %fusion.2 = (f32[64,16]{0,1:T(8,128)S(1)}, f32[512,64,16]{0,1,2:T(8,128)S(1)}) fusion(pred[64,512]{1,0:T(8,128)(4,1)S(1)} %broadcast_compare_fusion, bf16[1,64,16,576]{3,1,2,0:T(8,128)(2,1)} %get-tuple-element.279, bf16[1,1,512,576]{2,3,1,0:T(8,128)(2,1)S(1)} %constant_dynamic-slice_fusion), kind=kOutput, calls=%fused_computation.5 | convolution fusion | flops 605551616 | bytes 3903488 | tf_op jit(solution)/shard_map/while/body/eval_jaxpr/cond/branch_1_fun/pqhe,pke->pqhk/dot_general | solution.py:71
  195.7 2.2 copy.47
  203.4 9.1 %conditional.3 = ((f32[1,64,16]{1,2,0:T(8,128)S(1)}, f32[1,64,16]{1,2,0:T(8,128)S(1)}, f32[1,64,16,512]{3,2,1,0:T(8,128)S(1)})) conditional(s32[]{:T(128)} %bitcast.97, (f32[1,64,16]{1,2,0:T(8,128)S(1)}, f32[1,64,16]{1,2,0:T(8,128)S(1)}, f32[1,64,16,512]{3,2,1,0:T(8,128)S(1)}) %tuple.70, (s32[1,512]{1,0:T(1,128)S(1)}, s32[1,1,64]{2,1,0:T(1,128)S(1)}, ...), branch_computations={%region_4.0_spmd, %region_5.7_spmd} | conditional | flops 1146129408 | bytes 17668416 | solution.py:99
  204.7 2.5 %fusion.2 = (f32[64,16]{0,1:T(8,128)S(1)}, f32[512,64,16]{0,1,2:T(8,128)S(1)}) fusion(pred[64,512]{1,0:T(8,128)(4,1)S(1)} %broadcast_compare_fusion, bf16[1,64,16,576]{3,1,2,0:T(8,128)(2,1)} %get-tuple-element.279, bf16[1,1,512,576]{2,3,1,0:T(8,128)(2,1)S(1)} %constant_dynamic-slice_fusion), kind=kOutput, calls=%fused_computation.5 | convolution fusion | flops 605551616 | bytes 3903488 | tf_op jit(solution)/shard_map/while/body/eval_jaxpr/cond/branch_1_fun/pqhe,pke->pqhk/dot_general | solution.py:71
  210.2 2.2 bitcast_add_fusion
  215.7 9.0 %conditional.3 = ((f32[1,64,16]{1,2,0:T(8,128)S(1)}, f32[1,64,16]{1,2,0:T(8,128)S(1)}, f32[1,64,16,512]{3,2,1,0:T(8,128)S(1)})) conditional(s32[]{:T(128)} %bitcast.97, (f32[1,64,16]{1,2,0:T(8,128)S(1)}, f32[1,64,16]{1,2,0:T(8,128)S(1)}, f32[1,64,16,512]{3,2,1,0:T(8,128)S(1)}) %tuple.70, (s32[1,512]{1,0:T(1,128)S(1)}, s32[1,1,64]{2,1,0:T(1,128)S(1)}, ...), branch_computations={%region_4.0_spmd, %region_5.7_spmd} | conditional | flops 1146129408 | bytes 17668416 | solution.py:99
  216.9 2.5 %fusion.2 = (f32[64,16]{0,1:T(8,128)S(1)}, f32[512,64,16]{0,1,2:T(8,128)S(1)}) fusion(pred[64,512]{1,0:T(8,128)(4,1)S(1)} %broadcast_compare_fusion, bf16[1,64,16,576]{3,1,2,0:T(8,128)(2,1)} %get-tuple-element.279, bf16[1,1,512,576]{2,3,1,0:T(8,128)(2,1)S(1)} %constant_dynamic-slice_fusion), kind=kOutput, calls=%fused_computation.5 | convolution fusion | flops 605551616 | bytes 3903488 | tf_op jit(solution)/shard_map/while/body/eval_jaxpr/cond/branch_1_fun/pqhe,pke->pqhk/dot_general | solution.py:71
  225.1 2.4 %fusion.26 = bf16[1,64,16,128]{3,1,2,0:T(8,128)(2,1)S(1)} fusion(bf16[512,16,256]{0,2,1:T(8,128)(2,1)} %bitcast.100, bf16[64,16,512]{2,1,0:T(8,128)(2,1)S(1)} %fusion.30), kind=kOutput, calls=%fused_computation.34 | convolution fusion | flops 134348800 | bytes 3407872 | tf_op jit(solution)/shard_map/pqhl,lhv->pqhv/dot_general | solution.py:103
  227.7 5.7 %fusion.12 = bf16[1,1,64,2048]{3,2,1,0:T(8,128)(2,1)} fusion(bf16[2048,2048]{1,0:T(8,128)(2,1)} %all-gather.7.cloned.1.call-done, bf16[8,8,16,128]{3,2,1,0:T(8,128)(2,1)S(1)} %bitcast.105), kind=kOutput, calls=%fused_computation.24 | convolution fusion | flops 537001984 | bytes 8912896 | tf_op jit(solution)/shard_map/dot_general | solution.py:108
  (159 shorter events, 65.1 us)
Async XLA Ops:
  7.2 16.2 %copy-start.5 = (bf16[1,1,64,576]{3,2,1,0:T(8,128)(2,1)S(1)}, bf16[1,1,64,576]{3,2,1,0:T(8,128)(2,1)}, u32[]{:S(2)}) copy-start(bf16[1,1,64,576]{3,2,1,0:T(8,128)(2,1)} %param.13) | copy-start | bytes 221188
  7.2 16.1 %copy-start.6 = (bf16[512]{0:T(512)(128)(2,1)S(1)}, bf16[512]{0:T(512)(128)(2,1)}, u32[]{:S(2)}) copy-start(bf16[512]{0:T(512)(128)(2,1)} %param.17) | copy-start | bytes 3076
  7.2 69.0 %all-gather.5.cloned.1.call-start = ((), (), s32[]{:S(2)}) async-start(), calls=%async_computation | async-start | bytes 4718592 | tf_op jit(solution)/shard_map/all_gather | solution.py:19
  18.1 8.4 %copy-start.4 = (bf16[1,1,64,3072]{3,2,1,0:T(8,128)(2,1)S(1)}, bf16[1,1,64,3072]{3,2,1,0:T(8,128)(2,1)}, u32[]{:S(2)}) copy-start(bf16[1,1,64,3072]{3,2,1,0:T(8,128)(2,1)} %param.12) | copy-start | bytes 1179652
  18.1 99.9 %all-gather.9.cloned.1.call-start = ((), (), s32[]{:S(2)}) async-start(), calls=%async_computation.2 | async-start | bytes 5898240 | tf_op jit(solution)/shard_map/all_gather | solution.py:92
  24.9 0.8 copy-start.1
  25.8 1.4 copy-start.2
  25.8 201.9 %all-gather.7.cloned.1.call-start = ((), (), s32[]{:S(2)}) async-start(), calls=%async_computation.1 | async-start | bytes 8650752 | tf_op jit(solution)/shard_map/all_gather | solution.py:107
  27.1 2.3 copy-start.3
  76.2 6.5 %slice-start = ((bf16[1,1,64,16,192]{4,3,2,1,0:T(8,128)(2,1)}), bf16[1,1,64,16,128]{4,3,2,1,0:T(8,128)(2,1)S(1)}, s32[]{:S(2)}) async-start(bf16[1,1,64,16,192]{4,3,2,1,0:T(8,128)(2,1)} %copy-done.3), calls=%async_computation.3 | async-start | bytes 524288 | tf_op jit(solution)/shard_map/slice | solution.py:56
  125.7 0.7 copy-start.7
  130.7 2.6 %copy-start = (bf16[1,1,512,576]{2,3,1,0:T(8,128)(2,1)}, bf16[1,1,512,576]{2,3,1,0:T(8,128)(2,1)S(1)}, u32[]{:S(2)}) copy-start(bf16[1,1,512,576]{2,3,1,0:T(8,128)(2,1)S(1)} %constant_dynamic-slice_fusion) | copy-start | bytes 1769476 | tf_op jit(solution)/shard_map/while/body/eval_jaxpr/cond
  143.0 2.7 %copy-start = (bf16[1,1,512,576]{2,3,1,0:T(8,128)(2,1)}, bf16[1,1,512,576]{2,3,1,0:T(8,128)(2,1)S(1)}, u32[]{:S(2)}) copy-start(bf16[1,1,512,576]{2,3,1,0:T(8,128)(2,1)S(1)} %constant_dynamic-slice_fusion) | copy-start | bytes 1769476 | tf_op jit(solution)/shard_map/while/body/eval_jaxpr/cond
  155.3 2.6 %copy-start = (bf16[1,1,512,576]{2,3,1,0:T(8,128)(2,1)}, bf16[1,1,512,576]{2,3,1,0:T(8,128)(2,1)S(1)}, u32[]{:S(2)}) copy-start(bf16[1,1,512,576]{2,3,1,0:T(8,128)(2,1)S(1)} %constant_dynamic-slice_fusion) | copy-start | bytes 1769476 | tf_op jit(solution)/shard_map/while/body/eval_jaxpr/cond
  167.5 2.6 %copy-start = (bf16[1,1,512,576]{2,3,1,0:T(8,128)(2,1)}, bf16[1,1,512,576]{2,3,1,0:T(8,128)(2,1)S(1)}, u32[]{:S(2)}) copy-start(bf16[1,1,512,576]{2,3,1,0:T(8,128)(2,1)S(1)} %constant_dynamic-slice_fusion) | copy-start | bytes 1769476 | tf_op jit(solution)/shard_map/while/body/eval_jaxpr/cond
  179.9 2.6 %copy-start = (bf16[1,1,512,576]{2,3,1,0:T(8,128)(2,1)}, bf16[1,1,512,576]{2,3,1,0:T(8,128)(2,1)S(1)}, u32[]{:S(2)}) copy-start(bf16[1,1,512,576]{2,3,1,0:T(8,128)(2,1)S(1)} %constant_dynamic-slice_fusion) | copy-start | bytes 1769476 | tf_op jit(solution)/shard_map/while/body/eval_jaxpr/cond
  192.2 2.7 %copy-start = (bf16[1,1,512,576]{2,3,1,0:T(8,128)(2,1)}, bf16[1,1,512,576]{2,3,1,0:T(8,128)(2,1)S(1)}, u32[]{:S(2)}) copy-start(bf16[1,1,512,576]{2,3,1,0:T(8,128)(2,1)S(1)} %constant_dynamic-slice_fusion) | copy-start | bytes 1769476 | tf_op jit(solution)/shard_map/while/body/eval_jaxpr/cond
  204.6 2.6 %copy-start = (bf16[1,1,512,576]{2,3,1,0:T(8,128)(2,1)}, bf16[1,1,512,576]{2,3,1,0:T(8,128)(2,1)S(1)}, u32[]{:S(2)}) copy-start(bf16[1,1,512,576]{2,3,1,0:T(8,128)(2,1)S(1)} %constant_dynamic-slice_fusion) | copy-start | bytes 1769476 | tf_op jit(solution)/shard_map/while/body/eval_jaxpr/cond
  216.8 2.6 %copy-start = (bf16[1,1,512,576]{2,3,1,0:T(8,128)(2,1)}, bf16[1,1,512,576]{2,3,1,0:T(8,128)(2,1)S(1)}, u32[]{:S(2)}) copy-start(bf16[1,1,512,576]{2,3,1,0:T(8,128)(2,1)S(1)} %constant_dynamic-slice_fusion) | copy-start | bytes 1769476 | tf_op jit(solution)/shard_map/while/body/eval_jaxpr/cond
Sparse Core Ops, SparseCore 0:
  18.2 57.9 all-gather.4
  78.0 39.9 all-gather.8
  120.6 93.4 all-gather.6
where the time goes:
time: 242 us; the launch traced here: 240 us
  waiting for transfers between devices  79.4 us (33%)
  local copies, waits for them, and re-layouts  52.4 us (22%)
  matrix products  48.2 us (20%)
  other arithmetic  24.2 us (10%)
  between operations  14 us (6%)
  blocking collectives  10.8 us (4%)
  loops' own time  10.8 us (4%)
    all_gather x1, waiting for transfers between devices, whole_of(): whole = lax.all_gather(whole, axes[number], axis=dim, tiled=True)  46.8 us
    all_gather x1, waiting for transfers between devices, shards(): piece = lax.all_gather(blended, 'group', axis=1, tiled=True)  31.9 us
    dynamic_slice x16, local copies, waits for them, and re-layouts, one_group(): keys = lax.dynamic_slice_in_dim(piece, index, 1, 1)[:, 0]  26.8 us
    dot_general x8, matrix products, update(): jnp.einsum('pqhe,pke->pqhk', query_vec, keys, preferred_element_type=jnp....  20.2 us
    dot_general x8, matrix products, update(): jnp.einsum('pqhk,pkl->pqhl', probs.astype(jnp.bfloat16), keys[..., :LAT],...  17.9 us
    unnamed x18, local copies, waits for them, and re-layouts  11.4 us
    all_gather x1, blocking collectives, whole_of(): whole = lax.all_gather(whole, axes[number], axis=dim, tiled=True)  10.8 us
    another operation x1, loops' own time, shards(): lax.fori_loop(0, piece.shape[1], one_group, start_state)  10.2 us
  transfers between devices with their start and end apart: 3, of which 2 were waited for; matrix products, arithmetic and copies ran while one was open for 49% of the time, Pallas kernels for 0%

commit v1 on v0

--- a/solution.py
+++ b/solution.py
@@ -11,6 +11,27 @@
 DV = 128
 LAT = 512
 PROMPT = ("prompt_0", "prompt_1")
+
+
+def collect(x, axis, dim):
+    count, here, width = (lax.axis_size(axis), lax.axis_index(axis), x.shape[dim])
+    right = [(i, (i + 1) % count) for i in range(count)]
+    behind = [(i, (i - 1) % count) for i in range(count)]
+    filled = jnp.zeros((*x.shape[:dim], count * width, *x.shape[dim + 1 :]), x.dtype)
+    filled = lax.dynamic_update_slice_in_dim(filled, x, here * width, axis=dim)
+    from_left = from_right = x
+    halfway = count // 2
+    for turn in range(1, halfway + 1):
+        from_left = lax.ppermute(from_left, axis, right)
+        filled = lax.dynamic_update_slice_in_dim(
+            filled, from_left, (here - turn) % count * width, axis=dim
+        )
+        if turn < count - halfway:
+            from_right = lax.ppermute(from_right, axis, behind)
+            filled = lax.dynamic_update_slice_in_dim(
+                filled, from_right, (here + turn) % count * width, axis=dim
+            )
+    return filled
 
 
 def whole_of(array, axes, dim):
@@ -89,7 +110,7 @@
         jnp.zeros((prompts, rows, H), jnp.float32),
         jnp.zeros((prompts, rows, H, LAT), jnp.float32),
     )
-    piece = lax.all_gather(blended, "group", axis=1, tiled=True)
+    piece = collect(blended, "group", 1)
 
     def one_group(index, carry):
         keys = lax.dynamic_slice_in_dim(piece, index, 1, 1)[:, 0]

time: 242 us -> 201 us (0.83)
  the two profiles are of different devices: /device:TPU:57 before, /device:TPU:4 now
where the time goes in v1:
time: 201 us; the launch traced here: 199 us
  local copies, waits for them, and re-layouts  51.9 us (26%)
  matrix products  48.3 us (24%)
  waiting for transfers between devices  30.9 us (15%)
  other arithmetic  22.4 us (11%)
  blocking collectives  15.1 us (8%)
  between operations  14.3 us (7%)
  loops' own time  10.4 us (5%)
  starting transfers between devices  5.9 us (3%)
    dynamic_slice x16, local copies, waits for them, and re-layouts, one_group(): keys = lax.dynamic_slice_in_dim(piece, index, 1, 1)[:, 0]  26.2 us
    dot_general x8, matrix products, update(): jnp.einsum('pqhe,pke->pqhk', query_vec, keys, preferred_element_type=jnp....  20.3 us
    ppermute x4, waiting for transfers between devices, collect(): from_left = lax.ppermute(from_left, axis, right)  18 us
    dot_general x8, matrix products, update(): jnp.einsum('pqhk,pkl->pqhl', probs.astype(jnp.bfloat16), keys[..., :LAT],...  17.9 us
    all_gather x1, blocking collectives, whole_of(): whole = lax.all_gather(whole, axes[number], axis=dim, tiled=True)  15.1 us
    all_gather x1, waiting for transfers between devices, whole_of(): whole = lax.all_gather(whole, axes[number], axis=dim, tiled=True)  10.4 us
    another operation x1, loops' own time, shards(): lax.fori_loop(0, piece.shape[1], one_group, start_state)  9.77 us
    all_gather x1, local copies, waits for them, and re-layouts, whole_of(): whole = lax.all_gather(whole, axes[number], axis=dim, tiled=True)  6.48 us
  transfers between devices with their start and end apart: 9, of which 6 were waited for; matrix products, arithmetic and copies ran while one was open for 59% of the time, Pallas kernels for 0%

profile of v1, /device:TPU:4, one launch (start us, length us, event | category | flops | bytes accessed | tf_op | source)
XLA Modules:
  0.0 199.3 jit_solution(3622878935636186669)
XLA Ops:
  7.2 15.1 %all_gather.9 = bf16[64,4096]{1,0:T(8,128)(2,1)} all-gather(bf16[16,4096]{1,0:T(8,128)(2,1)} %param.18), channel_id=1, replica_groups=mesh['group'=8,'prompt_0'=8,'prompt_1'=4] {'prompt_1'}, dimensions={0}, use_global_device_ids=true | all-gather | bytes 655360 | tf_op jit(solution)/shard_map/all_gather | solution.py:40
  31.8 7.6 %collective-permute-done = bf16[1,1,512,576]{2,3,1,0:T(8,128)(2,1)S(1)} collective-permute-done((bf16[1,1,512,576]{2,3,1,0:T(8,128)(2,1)S(1)}, bf16[1,1,512,576]{2,3,1,0:T(8,128)(2,1)S(1)}, u32[]{:S(2)}, u32[]{:S(2)}) %collective-permute-start) | collective-permute-done | bytes 589856 | tf_op jit(solution)/shard_map/ppermute | solution.py:25
  43.6 2.6 %broadcast_in_dim.59 = bf16[1,8,512,576]{2,3,1,0:T(8,128)(2,1)} broadcast(bf16[]{:T(256)} %constant.130.clone.1), dimensions={} | broadcast | bytes 4718594 | tf_op jit(solution)/shard_map/broadcast_in_dim | solution.py:20
  51.0 2.3 %collective-permute-start.5 = (bf16[1,1,512,576]{2,3,1,0:T(8,128)(2,1)S(1)}, bf16[1,1,512,576]{2,3,1,0:T(8,128)(2,1)S(1)}, u32[]{:S(2)}, u32[]{:S(2)}) collective-permute-start(bf16[1,1,512,576]{2,3,1,0:T(8,128)(2,1)S(1)} %collective-permute-done.3), channel_id=1, source_target_pairs={{0,224},{32,0},{64,32},{96,64},{128,96},{160,128},{192,160},{224,1... | collective-permute-start | bytes 1769480 | tf_op jit(solution)/shard_map/ppermute | solution.py:30
  54.2 3.8 %collective-permute-done.4 = bf16[1,1,512,576]{2,3,1,0:T(8,128)(2,1)S(1)} collective-permute-done((bf16[1,1,512,576]{2,3,1,0:T(8,128)(2,1)S(1)}, bf16[1,1,512,576]{2,3,1,0:T(8,128)(2,1)S(1)}, u32[]{:S(2)}, u32[]{:S(2)}) %collective-permute-start.4) | collective-permute-done | bytes 589856 | tf_op jit(solution)/shard_map/ppermute | solution.py:25
  62.3 5.0 %collective-permute-done.6 = bf16[1,1,512,576]{2,3,1,0:T(8,128)(2,1)S(1)} collective-permute-done((bf16[1,1,512,576]{2,3,1,0:T(8,128)(2,1)S(1)}, bf16[1,1,512,576]{2,3,1,0:T(8,128)(2,1)S(1)}, u32[]{:S(2)}, u32[]{:S(2)}) %collective-permute-start.6) | collective-permute-done | bytes 589856 | tf_op jit(solution)/shard_map/ppermute | solution.py:25
  68.2 10.4 %all-gather.3.cloned.1.call-done = bf16[512,4096]{1,0:T(8,128)(2,1)} async-done(((bf16[64,4096]{1,0:T(8,128)(2,1)}), bf16[512,4096]{1,0:T(8,128)(2,1)}) %all-gather.3.cloned.1.call-update) | async-done | bytes 4194320 | tf_op jit(solution)/shard_map/all_gather | solution.py:40
  78.6 6.5 %copy.64 = bf16[512,4096]{0,1:T(8,128)(2,1)} copy(bf16[512,4096]{1,0:T(8,128)(2,1)} %all-gather.3.cloned.1.call-done) | data formatting | bytes 8388608 | tf_op jit(solution)/shard_map/all_gather | solution.py:40
  88.8 95.1 %while.20 = (s32[]{:T(128)}, f32[1,64,16]{1,2,0:T(8,128)S(1)}, f32[1,64,16]{1,2,0:T(8,128)S(1)}, f32[1,64,16,512]{3,2,1,0:T(8,128)S(1)}, s32[1,8]{1,0:T(1,128)S(...) while((s32[]{:T(128)}, f32[1,64,16]{1,2,0:T(8,128)S(1)}, ...), condition=%wide.region_8.9_spmd.clone, body=%wide.region_3.8_spmd.clone.sunk | while | flops 1146129920 | bytes 17670692 | solution.py:122
  91.6 9.1 %conditional.3 = ((f32[1,64,16]{1,2,0:T(8,128)S(1)}, f32[1,64,16]{1,2,0:T(8,128)S(1)}, f32[1,64,16,512]{3,2,1,0:T(8,128)S(1)})) conditional(s32[]{:T(128)} %bitcast.96, (f32[1,64,16]{1,2,0:T(8,128)S(1)}, f32[1,64,16]{1,2,0:T(8,128)S(1)}, f32[1,64,16,512]{3,2,1,0:T(8,128)S(1)}) %tuple.66, (s32[1,512]{1,0:T(1,128)S(1)}, s32[1,1,64]{2,1,0:T(1,128)S(1)}, ...), branch_computations={%region_4.4_spmd, %region_5.0_spmd} | conditional | flops 1146129408 | bytes 17668416 | solution.py:120
  92.9 2.5 %fusion.2 = (f32[64,16]{0,1:T(8,128)S(1)}, f32[512,64,16]{0,1,2:T(8,128)S(1)}) fusion(pred[64,512]{1,0:T(8,128)(4,1)S(1)} %broadcast_compare_fusion, bf16[1,64,16,576]{3,1,2,0:T(8,128)(2,1)} %get-tuple-element.279, bf16[1,1,512,576]{2,3,1,0:T(8,128)(2,1)S(1)} %constant_dynamic-slice_fusion), kind=kOutput, calls=%fused_computation.5 | convolution fusion | flops 605551616 | bytes 3903488 | tf_op jit(solution)/shard_map/while/body/eval_jaxpr/cond/branch_1_fun/pqhe,pke->pqhk/dot_general | solution.py:92
  98.4 2.2 %bitcast_add_fusion = f32[1,64,16,512]{3,2,1,0:T(8,128)S(1)} fusion(f32[1,64,16,512]{3,2,1,0:T(8,128)S(1)} %get-tuple-element.281, bf16[64,16,512]{2,0,1:T(8,128)(2,1)S(1)} %get-tuple-element.353, f32[64,16]{1,0:T(8,128)S(1)} %copy.54, bf16[1,512,576]{2,1,0:T(8,128)(2,1)} %bitcast.97), kind=kOutput, calls=%fused_computation.2 | convolution fusion | flops 537919488 | bytes 5771264 | tf_op jit(solution)/shard_map/while/body/eval_jaxpr/cond/branch_1_fun/pqhk,pkl->pqhl/dot_general | solution.py:100
  103.5 9.0 %conditional.3 = ((f32[1,64,16]{1,2,0:T(8,128)S(1)}, f32[1,64,16]{1,2,0:T(8,128)S(1)}, f32[1,64,16,512]{3,2,1,0:T(8,128)S(1)})) conditional(s32[]{:T(128)} %bitcast.96, (f32[1,64,16]{1,2,0:T(8,128)S(1)}, f32[1,64,16]{1,2,0:T(8,128)S(1)}, f32[1,64,16,512]{3,2,1,0:T(8,128)S(1)}) %tuple.66, (s32[1,512]{1,0:T(1,128)S(1)}, s32[1,1,64]{2,1,0:T(1,128)S(1)}, ...), branch_computations={%region_4.4_spmd, %region_5.0_spmd} | conditional | flops 1146129408 | bytes 17668416 | solution.py:120
  104.8 2.5 %fusion.2 = (f32[64,16]{0,1:T(8,128)S(1)}, f32[512,64,16]{0,1,2:T(8,128)S(1)}) fusion(pred[64,512]{1,0:T(8,128)(4,1)S(1)} %broadcast_compare_fusion, bf16[1,64,16,576]{3,1,2,0:T(8,128)(2,1)} %get-tuple-element.279, bf16[1,1,512,576]{2,3,1,0:T(8,128)(2,1)S(1)} %constant_dynamic-slice_fusion), kind=kOutput, calls=%fused_computation.5 | convolution fusion | flops 605551616 | bytes 3903488 | tf_op jit(solution)/shard_map/while/body/eval_jaxpr/cond/branch_1_fun/pqhe,pke->pqhk/dot_general | solution.py:92
  110.3 2.2 %bitcast_add_fusion = f32[1,64,16,512]{3,2,1,0:T(8,128)S(1)} fusion(f32[1,64,16,512]{3,2,1,0:T(8,128)S(1)} %get-tuple-element.281, bf16[64,16,512]{2,0,1:T(8,128)(2,1)S(1)} %get-tuple-element.353, f32[64,16]{1,0:T(8,128)S(1)} %copy.54, bf16[1,512,576]{2,1,0:T(8,128)(2,1)} %bitcast.97), kind=kOutput, calls=%fused_computation.2 | convolution fusion | flops 537919488 | bytes 5771264 | tf_op jit(solution)/shard_map/while/body/eval_jaxpr/cond/branch_1_fun/pqhk,pkl->pqhl/dot_general | solution.py:100
  115.4 9.0 %conditional.3 = ((f32[1,64,16]{1,2,0:T(8,128)S(1)}, f32[1,64,16]{1,2,0:T(8,128)S(1)}, f32[1,64,16,512]{3,2,1,0:T(8,128)S(1)})) conditional(s32[]{:T(128)} %bitcast.96, (f32[1,64,16]{1,2,0:T(8,128)S(1)}, f32[1,64,16]{1,2,0:T(8,128)S(1)}, f32[1,64,16,512]{3,2,1,0:T(8,128)S(1)}) %tuple.66, (s32[1,512]{1,0:T(1,128)S(1)}, s32[1,1,64]{2,1,0:T(1,128)S(1)}, ...), branch_computations={%region_4.4_spmd, %region_5.0_spmd} | conditional | flops 1146129408 | bytes 17668416 | solution.py:120
  116.6 2.5 %fusion.2 = (f32[64,16]{0,1:T(8,128)S(1)}, f32[512,64,16]{0,1,2:T(8,128)S(1)}) fusion(pred[64,512]{1,0:T(8,128)(4,1)S(1)} %broadcast_compare_fusion, bf16[1,64,16,576]{3,1,2,0:T(8,128)(2,1)} %get-tuple-element.279, bf16[1,1,512,576]{2,3,1,0:T(8,128)(2,1)S(1)} %constant_dynamic-slice_fusion), kind=kOutput, calls=%fused_computation.5 | convolution fusion | flops 605551616 | bytes 3903488 | tf_op jit(solution)/shard_map/while/body/eval_jaxpr/cond/branch_1_fun/pqhe,pke->pqhk/dot_general | solution.py:92
  122.2 2.2 %bitcast_add_fusion = f32[1,64,16,512]{3,2,1,0:T(8,128)S(1)} fusion(f32[1,64,16,512]{3,2,1,0:T(8,128)S(1)} %get-tuple-element.281, bf16[64,16,512]{2,0,1:T(8,128)(2,1)S(1)} %get-tuple-element.353, f32[64,16]{1,0:T(8,128)S(1)} %copy.54, bf16[1,512,576]{2,1,0:T(8,128)(2,1)} %bitcast.97), kind=kOutput, calls=%fused_computation.2 | convolution fusion | flops 537919488 | bytes 5771264 | tf_op jit(solution)/shard_map/while/body/eval_jaxpr/cond/branch_1_fun/pqhk,pkl->pqhl/dot_general | solution.py:100
  127.3 9.0 %conditional.3 = ((f32[1,64,16]{1,2,0:T(8,128)S(1)}, f32[1,64,16]{1,2,0:T(8,128)S(1)}, f32[1,64,16,512]{3,2,1,0:T(8,128)S(1)})) conditional(s32[]{:T(128)} %bitcast.96, (f32[1,64,16]{1,2,0:T(8,128)S(1)}, f32[1,64,16]{1,2,0:T(8,128)S(1)}, f32[1,64,16,512]{3,2,1,0:T(8,128)S(1)}) %tuple.66, (s32[1,512]{1,0:T(1,128)S(1)}, s32[1,1,64]{2,1,0:T(1,128)S(1)}, ...), branch_computations={%region_4.4_spmd, %region_5.0_spmd} | conditional | flops 1146129408 | bytes 17668416 | solution.py:120
  128.5 2.5 %fusion.2 = (f32[64,16]{0,1:T(8,128)S(1)}, f32[512,64,16]{0,1,2:T(8,128)S(1)}) fusion(pred[64,512]{1,0:T(8,128)(4,1)S(1)} %broadcast_compare_fusion, bf16[1,64,16,576]{3,1,2,0:T(8,128)(2,1)} %get-tuple-element.279, bf16[1,1,512,576]{2,3,1,0:T(8,128)(2,1)S(1)} %constant_dynamic-slice_fusion), kind=kOutput, calls=%fused_computation.5 | convolution fusion | flops 605551616 | bytes 3903488 | tf_op jit(solution)/shard_map/while/body/eval_jaxpr/cond/branch_1_fun/pqhe,pke->pqhk/dot_general | solution.py:92
  139.1 9.1 %conditional.3 = ((f32[1,64,16]{1,2,0:T(8,128)S(1)}, f32[1,64,16]{1,2,0:T(8,128)S(1)}, f32[1,64,16,512]{3,2,1,0:T(8,128)S(1)})) conditional(s32[]{:T(128)} %bitcast.96, (f32[1,64,16]{1,2,0:T(8,128)S(1)}, f32[1,64,16]{1,2,0:T(8,128)S(1)}, f32[1,64,16,512]{3,2,1,0:T(8,128)S(1)}) %tuple.66, (s32[1,512]{1,0:T(1,128)S(1)}, s32[1,1,64]{2,1,0:T(1,128)S(1)}, ...), branch_computations={%region_4.4_spmd, %region_5.0_spmd} | conditional | flops 1146129408 | bytes 17668416 | solution.py:120
  140.3 2.6 %fusion.2 = (f32[64,16]{0,1:T(8,128)S(1)}, f32[512,64,16]{0,1,2:T(8,128)S(1)}) fusion(pred[64,512]{1,0:T(8,128)(4,1)S(1)} %broadcast_compare_fusion, bf16[1,64,16,576]{3,1,2,0:T(8,128)(2,1)} %get-tuple-element.279, bf16[1,1,512,576]{2,3,1,0:T(8,128)(2,1)S(1)} %constant_dynamic-slice_fusion), kind=kOutput, calls=%fused_computation.5 | convolution fusion | flops 605551616 | bytes 3903488 | tf_op jit(solution)/shard_map/while/body/eval_jaxpr/cond/branch_1_fun/pqhe,pke->pqhk/dot_general | solution.py:92
  145.9 2.3 %bitcast_add_fusion = f32[1,64,16,512]{3,2,1,0:T(8,128)S(1)} fusion(f32[1,64,16,512]{3,2,1,0:T(8,128)S(1)} %get-tuple-element.281, bf16[64,16,512]{2,0,1:T(8,128)(2,1)S(1)} %get-tuple-element.353, f32[64,16]{1,0:T(8,128)S(1)} %copy.54, bf16[1,512,576]{2,1,0:T(8,128)(2,1)} %bitcast.97), kind=kOutput, calls=%fused_computation.2 | convolution fusion | flops 537919488 | bytes 5771264 | tf_op jit(solution)/shard_map/while/body/eval_jaxpr/cond/branch_1_fun/pqhk,pkl->pqhl/dot_general | solution.py:100
  151.0 9.1 %conditional.3 = ((f32[1,64,16]{1,2,0:T(8,128)S(1)}, f32[1,64,16]{1,2,0:T(8,128)S(1)}, f32[1,64,16,512]{3,2,1,0:T(8,128)S(1)})) conditional(s32[]{:T(128)} %bitcast.96, (f32[1,64,16]{1,2,0:T(8,128)S(1)}, f32[1,64,16]{1,2,0:T(8,128)S(1)}, f32[1,64,16,512]{3,2,1,0:T(8,128)S(1)}) %tuple.66, (s32[1,512]{1,0:T(1,128)S(1)}, s32[1,1,64]{2,1,0:T(1,128)S(1)}, ...), branch_computations={%region_4.4_spmd, %region_5.0_spmd} | conditional | flops 1146129408 | bytes 17668416 | solution.py:120
  152.3 2.6 %fusion.2 = (f32[64,16]{0,1:T(8,128)S(1)}, f32[512,64,16]{0,1,2:T(8,128)S(1)}) fusion(pred[64,512]{1,0:T(8,128)(4,1)S(1)} %broadcast_compare_fusion, bf16[1,64,16,576]{3,1,2,0:T(8,128)(2,1)} %get-tuple-element.279, bf16[1,1,512,576]{2,3,1,0:T(8,128)(2,1)S(1)} %constant_dynamic-slice_fusion), kind=kOutput, calls=%fused_computation.5 | convolution fusion | flops 605551616 | bytes 3903488 | tf_op jit(solution)/shard_map/while/body/eval_jaxpr/cond/branch_1_fun/pqhe,pke->pqhk/dot_general | solution.py:92
  157.8 2.3 %bitcast_add_fusion = f32[1,64,16,512]{3,2,1,0:T(8,128)S(1)} fusion(f32[1,64,16,512]{3,2,1,0:T(8,128)S(1)} %get-tuple-element.281, bf16[64,16,512]{2,0,1:T(8,128)(2,1)S(1)} %get-tuple-element.353, f32[64,16]{1,0:T(8,128)S(1)} %copy.54, bf16[1,512,576]{2,1,0:T(8,128)(2,1)} %bitcast.97), kind=kOutput, calls=%fused_computation.2 | convolution fusion | flops 537919488 | bytes 5771264 | tf_op jit(solution)/shard_map/while/body/eval_jaxpr/cond/branch_1_fun/pqhk,pkl->pqhl/dot_general | solution.py:100
  163.0 9.0 %conditional.3 = ((f32[1,64,16]{1,2,0:T(8,128)S(1)}, f32[1,64,16]{1,2,0:T(8,128)S(1)}, f32[1,64,16,512]{3,2,1,0:T(8,128)S(1)})) conditional(s32[]{:T(128)} %bitcast.96, (f32[1,64,16]{1,2,0:T(8,128)S(1)}, f32[1,64,16]{1,2,0:T(8,128)S(1)}, f32[1,64,16,512]{3,2,1,0:T(8,128)S(1)}) %tuple.66, (s32[1,512]{1,0:T(1,128)S(1)}, s32[1,1,64]{2,1,0:T(1,128)S(1)}, ...), branch_computations={%region_4.4_spmd, %region_5.0_spmd} | conditional | flops 1146129408 | bytes 17668416 | solution.py:120
  164.2 2.5 %fusion.2 = (f32[64,16]{0,1:T(8,128)S(1)}, f32[512,64,16]{0,1,2:T(8,128)S(1)}) fusion(pred[64,512]{1,0:T(8,128)(4,1)S(1)} %broadcast_compare_fusion, bf16[1,64,16,576]{3,1,2,0:T(8,128)(2,1)} %get-tuple-element.279, bf16[1,1,512,576]{2,3,1,0:T(8,128)(2,1)S(1)} %constant_dynamic-slice_fusion), kind=kOutput, calls=%fused_computation.5 | convolution fusion | flops 605551616 | bytes 3903488 | tf_op jit(solution)/shard_map/while/body/eval_jaxpr/cond/branch_1_fun/pqhe,pke->pqhk/dot_general | solution.py:92
  174.8 9.0 %conditional.3 = ((f32[1,64,16]{1,2,0:T(8,128)S(1)}, f32[1,64,16]{1,2,0:T(8,128)S(1)}, f32[1,64,16,512]{3,2,1,0:T(8,128)S(1)})) conditional(s32[]{:T(128)} %bitcast.96, (f32[1,64,16]{1,2,0:T(8,128)S(1)}, f32[1,64,16]{1,2,0:T(8,128)S(1)}, f32[1,64,16,512]{3,2,1,0:T(8,128)S(1)}) %tuple.66, (s32[1,512]{1,0:T(1,128)S(1)}, s32[1,1,64]{2,1,0:T(1,128)S(1)}, ...), branch_computations={%region_4.4_spmd, %region_5.0_spmd} | conditional | flops 1146129408 | bytes 17668416 | solution.py:120
  176.1 2.5 %fusion.2 = (f32[64,16]{0,1:T(8,128)S(1)}, f32[512,64,16]{0,1,2:T(8,128)S(1)}) fusion(pred[64,512]{1,0:T(8,128)(4,1)S(1)} %broadcast_compare_fusion, bf16[1,64,16,576]{3,1,2,0:T(8,128)(2,1)} %get-tuple-element.279, bf16[1,1,512,576]{2,3,1,0:T(8,128)(2,1)S(1)} %constant_dynamic-slice_fusion), kind=kOutput, calls=%fused_computation.5 | convolution fusion | flops 605551616 | bytes 3903488 | tf_op jit(solution)/shard_map/while/body/eval_jaxpr/cond/branch_1_fun/pqhe,pke->pqhk/dot_general | solution.py:92
  184.1 2.4 %fusion.26 = bf16[1,64,16,128]{3,1,2,0:T(8,128)(2,1)S(1)} fusion(bf16[512,16,256]{0,2,1:T(8,128)(2,1)} %bitcast.99, bf16[64,16,512]{2,1,0:T(8,128)(2,1)S(1)} %fusion.30), kind=kOutput, calls=%fused_computation.34 | convolution fusion | flops 134348800 | bytes 3407872 | tf_op jit(solution)/shard_map/pqhl,lhv->pqhv/dot_general | solution.py:124
  186.8 5.7 %fusion.12 = bf16[1,1,64,2048]{3,2,1,0:T(8,128)(2,1)} fusion(bf16[2048,2048]{1,0:T(8,128)(2,1)} %all-gather.5.cloned.1.call-done, bf16[8,8,16,128]{3,2,1,0:T(8,128)(2,1)S(1)} %bitcast.103), kind=kOutput, calls=%fused_computation.24 | convolution fusion | flops 537001984 | bytes 8912896 | tf_op jit(solution)/shard_map/dot_general | solution.py:129
  (174 shorter events, 81.7 us)
Async XLA Ops:
  7.2 21.1 %copy-start.3 = (bf16[1,1,64,576]{3,2,1,0:T(8,128)(2,1)S(1)}, bf16[1,1,64,576]{3,2,1,0:T(8,128)(2,1)}, u32[]{:S(2)}) copy-start(bf16[1,1,64,576]{3,2,1,0:T(8,128)(2,1)} %param.13) | copy-start | bytes 221188
  7.2 21.0 %copy-start.4 = (bf16[512]{0:T(512)(128)(2,1)S(1)}, bf16[512]{0:T(512)(128)(2,1)}, u32[]{:S(2)}) copy-start(bf16[512]{0:T(512)(128)(2,1)} %param.17) | copy-start | bytes 3076
  7.2 71.5 %all-gather.3.cloned.1.call-start = ((), (), s32[]{:S(2)}) async-start(), calls=%async_computation | async-start | bytes 4718592 | tf_op jit(solution)/shard_map/all_gather | solution.py:40
  22.3 164.4 %all-gather.5.cloned.1.call-start = ((), (), s32[]{:S(2)}) async-start(), calls=%async_computation.1 | async-start | bytes 8650752 | tf_op jit(solution)/shard_map/all_gather | solution.py:128
  30.1 16.2 %copy-start.1 = (bf16[1,1,512,576]{2,3,1,0:T(8,128)(2,1)}, bf16[1,1,512,576]{2,3,1,0:T(8,128)(2,1)S(1)}, u32[]{:S(2)}) copy-start(bf16[1,1,512,576]{2,3,1,0:T(8,128)(2,1)S(1)} %copy.61) | copy-start | bytes 1769476
  30.1 9.3 %collective-permute-start = (bf16[1,1,512,576]{2,3,1,0:T(8,128)(2,1)S(1)}, bf16[1,1,512,576]{2,3,1,0:T(8,128)(2,1)S(1)}, u32[]{:S(2)}, u32[]{:S(2)}) collective-permute-start(bf16[1,1,512,576]{2,3,1,0:T(8,128)(2,1)S(1)} %copy.61), channel_id=1, source_target_pairs={{0,32},{32,64},{64,96},{96,128},{128,160},{160,192},{192,224},{224... | collective-permute-start | bytes 1769480 | tf_op jit(solution)/shard_map/ppermute | solution.py:25
  30.1 11.7 %collective-permute-start.1 = (bf16[1,1,512,576]{2,3,1,0:T(8,128)(2,1)S(1)}, bf16[1,1,512,576]{2,3,1,0:T(8,128)(2,1)S(1)}, u32[]{:S(2)}, u32[]{:S(2)}) collective-permute-start(bf16[1,1,512,576]{2,3,1,0:T(8,128)(2,1)S(1)} %copy.61), channel_id=1, source_target_pairs={{0,224},{32,0},{64,32},{96,64},{128,96},{160,128},{192,160},{224,1... | collective-permute-start | bytes 1769480 | tf_op jit(solution)/shard_map/ppermute | solution.py:30
  39.4 9.3 %collective-permute-start.2 = (bf16[1,1,512,576]{2,3,1,0:T(8,128)(2,1)S(1)}, bf16[1,1,512,576]{2,3,1,0:T(8,128)(2,1)S(1)}, u32[]{:S(2)}, u32[]{:S(2)}) collective-permute-start(bf16[1,1,512,576]{2,3,1,0:T(8,128)(2,1)S(1)} %collective-permute-done), channel_id=1, source_target_pairs={{0,32},{32,64},{64,96},{96,128},{128,160},{160,192},{192,224},{224... | collective-permute-start | bytes 1769480 | tf_op jit(solution)/shard_map/ppermute | solution.py:25
  41.0 5.2 %copy-start.2 = (bf16[1,1,64,16,192]{4,3,2,1,0:T(8,128)(2,1)}, bf16[1,1,64,16,192]{4,3,2,1,0:T(8,128)(2,1)S(1)}, u32[]{:S(2)}) copy-start(bf16[1,1,64,16,192]{4,3,2,1,0:T(8,128)(2,1)S(1)} %reshape.418) | copy-start | bytes 1179652
  41.8 9.2 %collective-permute-start.3 = (bf16[1,1,512,576]{2,3,1,0:T(8,128)(2,1)S(1)}, bf16[1,1,512,576]{2,3,1,0:T(8,128)(2,1)S(1)}, u32[]{:S(2)}, u32[]{:S(2)}) collective-permute-start(bf16[1,1,512,576]{2,3,1,0:T(8,128)(2,1)S(1)} %collective-permute-done.1), channel_id=1, source_target_pairs={{0,224},{32,0},{64,32},{96,64},{128,96},{160,128},{192,160},{224,1... | collective-permute-start | bytes 1769480 | tf_op jit(solution)/shard_map/ppermute | solution.py:30
  48.7 9.3 %collective-permute-start.4 = (bf16[1,1,512,576]{2,3,1,0:T(8,128)(2,1)S(1)}, bf16[1,1,512,576]{2,3,1,0:T(8,128)(2,1)S(1)}, u32[]{:S(2)}, u32[]{:S(2)}) collective-permute-start(bf16[1,1,512,576]{2,3,1,0:T(8,128)(2,1)S(1)} %collective-permute-done.2), channel_id=1, source_target_pairs={{0,32},{32,64},{64,96},{96,128},{128,160},{160,192},{192,224},{224... | collective-permute-start | bytes 1769480 | tf_op jit(solution)/shard_map/ppermute | solution.py:25
  51.0 10.4 %collective-permute-start.5 = (bf16[1,1,512,576]{2,3,1,0:T(8,128)(2,1)S(1)}, bf16[1,1,512,576]{2,3,1,0:T(8,128)(2,1)S(1)}, u32[]{:S(2)}, u32[]{:S(2)}) collective-permute-start(bf16[1,1,512,576]{2,3,1,0:T(8,128)(2,1)S(1)} %collective-permute-done.3), channel_id=1, source_target_pairs={{0,224},{32,0},{64,32},{96,64},{128,96},{160,128},{192,160},{224,1... | collective-permute-start | bytes 1769480 | tf_op jit(solution)/shard_map/ppermute | solution.py:30
  58.0 9.3 %collective-permute-start.6 = (bf16[1,1,512,576]{2,3,1,0:T(8,128)(2,1)S(1)}, bf16[1,1,512,576]{2,3,1,0:T(8,128)(2,1)S(1)}, u32[]{:S(2)}, u32[]{:S(2)}) collective-permute-start(bf16[1,1,512,576]{2,3,1,0:T(8,128)(2,1)S(1)} %collective-permute-done.4), channel_id=1, source_target_pairs={{0,32},{32,64},{64,96},{96,128},{128,160},{160,192},{192,224},{224... | collective-permute-start | bytes 1769480 | tf_op jit(solution)/shard_map/ppermute | solution.py:25
  68.2 16.9 %slice-start = ((bf16[1,1,64,16,192]{4,3,2,1,0:T(8,128)(2,1)}), bf16[1,1,64,16,128]{4,3,2,1,0:T(8,128)(2,1)S(1)}, s32[]{:S(2)}) async-start(bf16[1,1,64,16,192]{4,3,2,1,0:T(8,128)(2,1)} %copy-done.2), calls=%async_computation.2 | async-start | bytes 524288 | tf_op jit(solution)/shard_map/slice | solution.py:77
  87.2 1.6 copy-start.5
  92.8 2.7 %copy-start = (bf16[1,1,512,576]{2,3,1,0:T(8,128)(2,1)}, bf16[1,1,512,576]{2,3,1,0:T(8,128)(2,1)S(1)}, u32[]{:S(2)}) copy-start(bf16[1,1,512,576]{2,3,1,0:T(8,128)(2,1)S(1)} %constant_dynamic-slice_fusion) | copy-start | bytes 1769476 | tf_op jit(solution)/shard_map/while/body/eval_jaxpr/cond
  104.7 2.6 %copy-start = (bf16[1,1,512,576]{2,3,1,0:T(8,128)(2,1)}, bf16[1,1,512,576]{2,3,1,0:T(8,128)(2,1)S(1)}, u32[]{:S(2)}) copy-start(bf16[1,1,512,576]{2,3,1,0:T(8,128)(2,1)S(1)} %constant_dynamic-slice_fusion) | copy-start | bytes 1769476 | tf_op jit(solution)/shard_map/while/body/eval_jaxpr/cond
  116.5 2.6 %copy-start = (bf16[1,1,512,576]{2,3,1,0:T(8,128)(2,1)}, bf16[1,1,512,576]{2,3,1,0:T(8,128)(2,1)S(1)}, u32[]{:S(2)}) copy-start(bf16[1,1,512,576]{2,3,1,0:T(8,128)(2,1)S(1)} %constant_dynamic-slice_fusion) | copy-start | bytes 1769476 | tf_op jit(solution)/shard_map/while/body/eval_jaxpr/cond
  128.4 2.6 %copy-start = (bf16[1,1,512,576]{2,3,1,0:T(8,128)(2,1)}, bf16[1,1,512,576]{2,3,1,0:T(8,128)(2,1)S(1)}, u32[]{:S(2)}) copy-start(bf16[1,1,512,576]{2,3,1,0:T(8,128)(2,1)S(1)} %constant_dynamic-slice_fusion) | copy-start | bytes 1769476 | tf_op jit(solution)/shard_map/while/body/eval_jaxpr/cond
  140.2 2.7 %copy-start = (bf16[1,1,512,576]{2,3,1,0:T(8,128)(2,1)}, bf16[1,1,512,576]{2,3,1,0:T(8,128)(2,1)S(1)}, u32[]{:S(2)}) copy-start(bf16[1,1,512,576]{2,3,1,0:T(8,128)(2,1)S(1)} %constant_dynamic-slice_fusion) | copy-start | bytes 1769476 | tf_op jit(solution)/shard_map/while/body/eval_jaxpr/cond
  152.2 2.7 %copy-start = (bf16[1,1,512,576]{2,3,1,0:T(8,128)(2,1)}, bf16[1,1,512,576]{2,3,1,0:T(8,128)(2,1)S(1)}, u32[]{:S(2)}) copy-start(bf16[1,1,512,576]{2,3,1,0:T(8,128)(2,1)S(1)} %constant_dynamic-slice_fusion) | copy-start | bytes 1769476 | tf_op jit(solution)/shard_map/while/body/eval_jaxpr/cond
  164.1 2.6 %copy-start = (bf16[1,1,512,576]{2,3,1,0:T(8,128)(2,1)}, bf16[1,1,512,576]{2,3,1,0:T(8,128)(2,1)S(1)}, u32[]{:S(2)}) copy-start(bf16[1,1,512,576]{2,3,1,0:T(8,128)(2,1)S(1)} %constant_dynamic-slice_fusion) | copy-start | bytes 1769476 | tf_op jit(solution)/shard_map/while/body/eval_jaxpr/cond
  176.0 2.6 %copy-start = (bf16[1,1,512,576]{2,3,1,0:T(8,128)(2,1)}, bf16[1,1,512,576]{2,3,1,0:T(8,128)(2,1)S(1)}, u32[]{:S(2)}) copy-start(bf16[1,1,512,576]{2,3,1,0:T(8,128)(2,1)S(1)} %constant_dynamic-slice_fusion) | copy-start | bytes 1769476 | tf_op jit(solution)/shard_map/while/body/eval_jaxpr/cond
Sparse Core Ops, SparseCore 0:
  22.5 56.1 all-gather.2
  81.2 96.5 all-gather.4
